TPU v7x, 32 devices: a whole 2x2x4 slice. The times are simulated.
32 devices in a mesh: py: 4 (over z), pz: 8 (over y, x, core).
Axes of the slice: x: 2, y: 2, z: 4, core: 2. Of those that a mesh axis runs over, the one named last changes fastest.
Arguments:
- start: float32 [32, 64, 512], P('py', 'pz'), may hold values from -36 to 36
- coef_x: float32 [32, 64, 512], P('py', 'pz'), may hold values from 0.5 to 2
- coef_y: float32 [32, 64, 512], P('py', 'pz'), may hold values from 0.5 to 2
- coef_z: float32 [32, 64, 512], P('py', 'pz'), may hold values from 0.5 to 2
- shifts: float32 [8], replicated, may hold values from 0 to 14
Outputs:
- orthonormal: float32 [9, 32, 64, 512], P(None, 'py', 'pz')
- triangle: float32 [9, 9], replicated
All inputs are finite; a program needn't handle non-finite values.
Results may differ from a plain program's by a relative error of at most 0.0003.
Values sent between devices are 32-bit elements; how exact they have to be, the bound alone decides.
A program may use at most 128 MiB of HBM per device.

v0:
```python
import math

import jax
import jax.numpy as jnp
from jax import lax
from jax.sharding import PartitionSpec as P

step_scale = 0.125


def shifted(value, axis, by):
    devices = lax.axis_size(axis)
    pairs = [(i, i + by) for i in range(devices) if 0 <= i + by < devices]
    return lax.ppermute(value, axis, pairs)


def padded_2(block, sides, width):
    for axis, dim in sides:
        count = lax.axis_size(axis)
        forward = [(i, i + 1) for i in range(count - 1)]
        backward = [(target, source) for source, target in forward]
        low = lax.ppermute(
            lax.slice_in_dim(block, block.shape[dim] - width, None, axis=dim), axis, forward
        )
        high = lax.ppermute(lax.slice_in_dim(block, 0, width, axis=dim), axis, backward)
        block = jnp.concatenate([low, block, high], axis=dim)
    return block


def from_partner(value, axis, bit):
    return lax.ppermute(value, axis, [(i, i ^ 1 << bit) for i in range(lax.axis_size(axis))])


def below_cells(array, dim):
    edge = jnp.zeros_like(lax.slice_in_dim(array, 0, 1, axis=dim))
    return jnp.concatenate(
        [edge, lax.slice_in_dim(array, 0, array.shape[dim] - 1, axis=dim)], axis=dim
    )


def above_cells(array, dim):
    edge = jnp.zeros_like(lax.slice_in_dim(array, 0, 1, axis=dim))
    return jnp.concatenate([lax.slice_in_dim(array, 1, array.shape[dim], axis=dim), edge], axis=dim)


def stencil(padded, coef_x, coef_y, coef_z, below_x, below_y, below_z):
    centre = padded[1:-1, 1:-1]
    result = coef_x * (centre - above_cells(centre, 2)) + below_x * (
        centre - below_cells(centre, 2)
    )
    result = result + coef_y * (centre - padded[2:, 1:-1]) + below_y * (centre - padded[:-2, 1:-1])
    result = result + coef_z * (centre - padded[1:-1, 2:]) + below_z * (centre - padded[1:-1, :-2])
    return result


def forward(factor, vectors):
    count = factor.shape[0]
    solved = []
    for row in range(count):
        partial_sum = vectors[row]
        for inner in range(row):
            partial_sum = partial_sum - factor[inner, row] * solved[inner]
        solved.append(partial_sum / factor[row, row])
    return jnp.stack(solved)


def triangle_of(matrix):
    count, breadth = matrix.shape
    positions = jnp.arange(breadth)
    for column in range(count):
        current = matrix[column]
        masked = jnp.where(positions >= column, current, 0.0)
        length = jnp.sqrt(jnp.sum(masked * masked))
        alpha = -jnp.where(current[column] >= 0, 1.0, -1.0) * length
        reflector = masked - alpha * (positions == column).astype(jnp.float32)
        weight = jnp.sum(reflector * reflector)
        project = jnp.sum(matrix * reflector[None, :], axis=1)
        matrix = matrix - 2.0 / weight * project[:, None] * reflector[None, :]
    upper = jnp.triu(matrix[:, :count].T)
    signs = jnp.where(jnp.diagonal(upper) >= 0, 1.0, -1.0)
    return upper * signs[:, None]


def combine_pair(mine, other, upper_half):
    lower_part = jnp.where(upper_half, other, mine)
    upper_part = jnp.where(upper_half, mine, other)
    return triangle_of(jnp.concatenate([lower_part.T, upper_part.T], axis=1))


def on_device(start, coef_x, coef_y, coef_z, shifts):
    rows_y, rows_z, length_x = start.shape
    depth = shifts.shape[0]
    vectors = [start]
    edge_y = shifted(coef_y[-1:], "py", 1)
    edge_z = shifted(coef_z[:, -1:], "pz", 1)
    below_y = jnp.concatenate([edge_y, coef_y[:-1]], axis=0)
    below_z = jnp.concatenate([edge_z, coef_z[:, :-1]], axis=1)
    below_x = below_cells(coef_x, 2)
    current = start
    for level in range(depth):
        padded = padded_2(current, (("py", 0), ("pz", 1)), 1)
        image = stencil(padded, coef_x, coef_y, coef_z, below_x, below_y, below_z)
        current = (image - shifts[level] * current) * step_scale
        vectors.append(current)
    basis = jnp.stack(vectors)
    flat = basis.reshape(basis.shape[0], -1)
    total_cells = length_x * rows_y * rows_z * lax.axis_size("py") * lax.axis_size("pz")
    factor = triangle_of(flat)
    for bit in range(lax.axis_size("pz").bit_length() - 1):
        other = from_partner(factor, "pz", bit)
        factor = combine_pair(factor, other, lax.axis_index("pz") >> bit & 1 == 1)
    for bit in range(lax.axis_size("py").bit_length() - 1):
        other = from_partner(factor, "py", bit)
        factor = combine_pair(factor, other, lax.axis_index("py") >> bit & 1 == 1)
    triangle = factor / math.sqrt(total_cells)
    orthonormal = forward(triangle, flat).reshape(basis.shape)
    return (orthonormal, triangle)


def solution(mesh):
    placed = (
        P("py", "pz", None),
        P("py", "pz", None),
        P("py", "pz", None),
        P("py", "pz", None),
        P(),
    )
    return jax.shard_map(
        on_device,
        mesh=mesh,
        in_specs=placed,
        out_specs=(P(None, "py", "pz", None), P()),
        check_vma=False,
    )
```

profile of v0, /device:TPU:0, one launch (start us, length us, event | category | flops | bytes accessed | tf_op | source)
XLA Modules:
  0.0 1120.0 jit_solution(13705335487607373675)
XLA Ops:
  153.9 15.3 %multiply_subtract_fusion.7 = f32[9,32768]{0,1:T(8,128)S(1)} fusion(f32[9,32768]{0,1:T(8,128)} %copy.27, f32[9]{0:T(128)S(1)} %broadcast_multiply_fusion.65, f32[32768]{0:T(1024)S(1)} %select_subtract_fusion), kind=kLoop, calls=%fused_computation.45 | loop fusion | flops 589824 | bytes 2490404 | tf_op jit(solution)/shard_map/sub | solution.py:78
  193.8 18.1 %multiply_reduce_fusion.7 = f32[9]{0:T(128)S(1)} fusion(f32[32768]{0:T(1024)S(1)} %subtract_reduce_fusion.7, f32[9,32768]{0,1:T(8,128)} %copy.27, f32[32768]{0:T(1024)S(1)} %select_subtract_fusion, f32[9]{0:T(128)S(1)} %broadcast_multiply_fusion.65), kind=kLoop, calls=%fused_computation.41 | loop fusion | flops 1179639 | bytes 1441864 | tf_op jit(solution)/shard_map/reduce_sum | solution.py:77
  212.0 18.6 %multiply_subtract_fusion.6 = f32[9,32768]{0,1:T(8,128)S(1)} fusion(f32[9]{0:T(128)S(1)} %broadcast_multiply_fusion.64, f32[32768]{0:T(1024)S(1)} %subtract_reduce_fusion.7, f32[9,32768]{0,1:T(8,128)} %copy.27, f32[32768]{0:T(1024)S(1)} %select_subtract_fusion, f32[9]{0:T(128)S(1)} %broadcast_multiply_fusion.65), kind=kLoop, calls=%fused_computation.40 | loop fusion | flops 1179648 | bytes 2621512 | tf_op jit(solution)/shard_map/sub | solution.py:78
  243.0 11.7 %subtract_reduce_fusion.6 = f32[32768]{0:T(1024)S(1)} fusion(f32[9,32768]{0,1:T(8,128)} %copy-done.1, f32[]{:T(128)S(6)} %mul.3652), kind=kLoop, calls=%fused_computation.37 | loop fusion | flops 163840 | bytes 262148 | tf_op jit(solution)/shard_map/sub | solution.py:75
  255.3 16.8 %multiply_reduce_fusion.6 = f32[9]{0:T(128)S(1)} fusion(f32[32768]{0:T(1024)S(1)} %subtract_reduce_fusion.6, f32[32768]{0:T(1024)S(1)} %subtract_reduce_fusion.7, f32[9]{0:T(128)S(1)} %broadcast_multiply_fusion.64, f32[9,32768]{0,1:T(8,128)} %copy.27, f32[32768]{0:T(1024)S(1)} %select_subtract_fusion, f32[9]{0:T(128)S(1)} %broadcast_multiply_fusion.65), kind=kLoop, calls=%fused_computation.36 | loop fusion | flops 1769463 | bytes 1572972 | tf_op jit(solution)/shard_map/reduce_sum | solution.py:77
  272.2 20.6 %multiply_subtract_fusion.5 = f32[9,32768]{0,1:T(8,128)S(1)} fusion(f32[9]{0:T(128)S(1)} %broadcast_multiply_fusion.63, f32[32768]{0:T(1024)S(1)} %subtract_reduce_fusion.6, f32[32768]{0:T(1024)S(1)} %subtract_reduce_fusion.7, f32[9]{0:T(128)S(1)} %broadcast_multiply_fusion.64, f32[9,32768]{0,1:T(8,128)} %copy.27, f32[32768]{0:T(1024)S(1)} %select_subtract_fusion, ...), kind=kLoop, calls=%fused_computation.35 | loop fusion | flops 1769472 | bytes 2752620 | tf_op jit(solution)/shard_map/sub | solution.py:78
  305.1 11.5 %subtract_reduce_fusion.5 = f32[32768]{0:T(1024)S(1)} fusion(f32[9,32768]{0,1:T(8,128)} %copy-done.5, f32[]{:T(128)S(6)} %mul.3666), kind=kLoop, calls=%fused_computation.32 | loop fusion | flops 163840 | bytes 262148 | tf_op jit(solution)/shard_map/sub | solution.py:75
  317.3 21.1 %multiply_reduce_fusion.5 = f32[9]{0:T(128)S(1)} fusion(f32[32768]{0:T(1024)S(1)} %subtract_reduce_fusion.5, f32[32768]{0:T(1024)S(1)} %subtract_reduce_fusion.6, f32[9]{0:T(128)S(1)} %broadcast_multiply_fusion.63, f32[32768]{0:T(1024)S(1)} %subtract_reduce_fusion.7, f32[9]{0:T(128)S(1)} %broadcast_multiply_fusion.64, f32[9,32768]{0,1:T(8,128)} %copy.27, ...), kind=kLoop, calls=%fused_computation.31 | loop fusion | flops 2359287 | bytes 1704080 | tf_op jit(solution)/shard_map/reduce_sum | solution.py:77
  338.5 19.9 %multiply_subtract_fusion.4 = f32[9,32768]{0,1:T(8,128)S(1)} fusion(f32[9]{0:T(128)S(1)} %broadcast_multiply_fusion.62, f32[32768]{0:T(1024)S(1)} %subtract_reduce_fusion.5, f32[32768]{0:T(1024)S(1)} %subtract_reduce_fusion.6, f32[9]{0:T(128)S(1)} %broadcast_multiply_fusion.63, f32[32768]{0:T(1024)S(1)} %subtract_reduce_fusion.7, ...), kind=kLoop, calls=%fused_computation.30 | loop fusion | flops 2359296 | bytes 2883728 | tf_op jit(solution)/shard_map/sub | solution.py:78
  370.7 11.9 %subtract_reduce_fusion.4 = f32[32768]{0:T(1024)S(1)} fusion(f32[9,32768]{0,1:T(8,128)} %copy-done.6, f32[]{:T(128)S(6)} %mul.3680), kind=kLoop, calls=%fused_computation.27 | loop fusion | flops 163840 | bytes 262148 | tf_op jit(solution)/shard_map/sub | solution.py:75
  383.2 25.4 %multiply_reduce_fusion.4 = f32[9]{0:T(128)S(1)} fusion(f32[32768]{0:T(1024)S(1)} %subtract_reduce_fusion.4, f32[32768]{0:T(1024)S(1)} %subtract_reduce_fusion.5, f32[9]{0:T(128)S(1)} %broadcast_multiply_fusion.62, f32[32768]{0:T(1024)S(1)} %subtract_reduce_fusion.6, f32[9]{0:T(128)S(1)} %broadcast_multiply_fusion.63, f32[32768]{0:T(1024)S(1)} %subtract_reduce_fusion.7, ...), kind=kLoop, calls=%fused_computation.26 | loop fusion | flops 2949111 | bytes 1835188 | tf_op jit(solution)/shard_map/reduce_sum | solution.py:77
  408.7 24.2 %multiply_subtract_fusion.3 = f32[9,32768]{0,1:T(8,128)S(1)} fusion(f32[9]{0:T(128)S(1)} %broadcast_multiply_fusion.61, f32[32768]{0:T(1024)S(1)} %subtract_reduce_fusion.4, f32[32768]{0:T(1024)S(1)} %subtract_reduce_fusion.5, f32[9]{0:T(128)S(1)} %broadcast_multiply_fusion.62, f32[32768]{0:T(1024)S(1)} %subtract_reduce_fusion.6, ...), kind=kLoop, calls=%fused_computation.25 | loop fusion | flops 2949120 | bytes 3014836 | tf_op jit(solution)/shard_map/sub | solution.py:78
  457.4 29.8 %multiply_reduce_fusion.3 = f32[9]{0:T(128)S(1)} fusion(f32[32768]{0:T(1024)S(1)} %subtract_reduce_fusion.3, f32[32768]{0:T(1024)S(1)} %subtract_reduce_fusion.4, f32[9]{0:T(128)S(1)} %broadcast_multiply_fusion.61, f32[32768]{0:T(1024)S(1)} %subtract_reduce_fusion.5, f32[9]{0:T(128)S(1)} %broadcast_multiply_fusion.62, f32[32768]{0:T(1024)S(1)} %subtract_reduce_fusion.6, ...), kind=kLoop, calls=%fused_computation.21 | loop fusion | flops 3538935 | bytes 1966296 | tf_op jit(solution)/shard_map/reduce_sum | solution.py:77
  487.2 28.5 %multiply_subtract_fusion.2 = f32[9,32768]{0,1:T(8,128)S(1)} fusion(f32[9]{0:T(128)S(1)} %broadcast_multiply_fusion.60, f32[32768]{0:T(1024)S(1)} %subtract_reduce_fusion.3, f32[32768]{0:T(1024)S(1)} %subtract_reduce_fusion.4, f32[9]{0:T(128)S(1)} %broadcast_multiply_fusion.61, f32[32768]{0:T(1024)S(1)} %subtract_reduce_fusion.5, ...), kind=kLoop, calls=%fused_computation.20 | loop fusion | flops 3538944 | bytes 3145944 | tf_op jit(solution)/shard_map/sub | solution.py:78
  528.2 11.5 %subtract_reduce_fusion.2 = f32[32768]{0:T(1024)S(1)} fusion(f32[9,32768]{0,1:T(8,128)} %copy-done.3, f32[]{:T(128)S(6)} %mul.3708), kind=kLoop, calls=%fused_computation.17 | loop fusion | flops 163840 | bytes 262148 | tf_op jit(solution)/shard_map/sub | solution.py:75
  540.3 34.1 %multiply_reduce_fusion.2 = f32[9]{0:T(128)S(1)} fusion(f32[32768]{0:T(1024)S(1)} %subtract_reduce_fusion.2, f32[32768]{0:T(1024)S(1)} %subtract_reduce_fusion.3, f32[9]{0:T(128)S(1)} %broadcast_multiply_fusion.60, f32[32768]{0:T(1024)S(1)} %subtract_reduce_fusion.4, f32[9]{0:T(128)S(1)} %broadcast_multiply_fusion.61, f32[32768]{0:T(1024)S(1)} %subtract_reduce_fusion.5, ...), kind=kLoop, calls=%fused_computation.16 | loop fusion | flops 4128759 | bytes 2097404 | tf_op jit(solution)/shard_map/reduce_sum | solution.py:77
  574.4 32.8 %multiply_subtract_fusion.1 = f32[9,32768]{0,1:T(8,128)S(1)} fusion(f32[9]{0:T(128)S(1)} %broadcast_multiply_fusion.59, f32[32768]{0:T(1024)S(1)} %subtract_reduce_fusion.2, f32[32768]{0:T(1024)S(1)} %subtract_reduce_fusion.3, f32[9]{0:T(128)S(1)} %broadcast_multiply_fusion.60, f32[32768]{0:T(1024)S(1)} %subtract_reduce_fusion.4, ...), kind=kLoop, calls=%fused_computation.15 | loop fusion | flops 4128768 | bytes 3277052 | tf_op jit(solution)/shard_map/sub | solution.py:78
  631.7 38.4 %multiply_reduce_fusion.1 = f32[9]{0:T(128)S(1)} fusion(f32[32768]{0:T(1024)S(1)} %subtract_reduce_fusion.1, f32[32768]{0:T(1024)S(1)} %subtract_reduce_fusion.2, f32[9]{0:T(128)S(1)} %broadcast_multiply_fusion.59, f32[32768]{0:T(1024)S(1)} %subtract_reduce_fusion.3, f32[9]{0:T(128)S(1)} %broadcast_multiply_fusion.60, f32[32768]{0:T(1024)S(1)} %subtract_reduce_fusion.4, ...), kind=kLoop, calls=%fused_computation.11 | loop fusion | flops 4718583 | bytes 2228512 | tf_op jit(solution)/shard_map/reduce_sum | solution.py:77
  670.2 37.3 %multiply_subtract_fusion = f32[9,32768]{0,1:T(8,128)S(1)} fusion(f32[9]{0:T(128)S(1)} %broadcast_multiply_fusion.58, f32[32768]{0:T(1024)S(1)} %subtract_reduce_fusion.1, f32[32768]{0:T(1024)S(1)} %subtract_reduce_fusion.2, f32[9]{0:T(128)S(1)} %broadcast_multiply_fusion.59, f32[32768]{0:T(1024)S(1)} %subtract_reduce_fusion.3, ...), kind=kLoop, calls=%fused_computation.10 | loop fusion | flops 4718592 | bytes 3408160 | tf_op jit(solution)/shard_map/sub | solution.py:78
  731.4 43.1 %multiply_reduce_fusion = f32[9]{0:T(128)S(1)} fusion(f32[32768]{0:T(1024)S(1)} %subtract_reduce_fusion, f32[32768]{0:T(1024)S(1)} %subtract_reduce_fusion.1, f32[9]{0:T(128)S(1)} %broadcast_multiply_fusion.58, f32[32768]{0:T(1024)S(1)} %subtract_reduce_fusion.2, f32[9]{0:T(128)S(1)} %broadcast_multiply_fusion.59, f32[32768]{0:T(1024)S(1)} %subtract_reduce_fusion.3, ...), kind=kLoop, calls=%fused_computation.6 | loop fusion | flops 5308407 | bytes 2359620 | tf_op jit(solution)/shard_map/reduce_sum | solution.py:77
  1036.6 13.1 %bitcast_dynamic-update-slice_fusion.3 = f32[9,8,8,512]{3,2,1,0:T(8,128)S(1)} fusion(f32[9,8,8,512]{3,2,1,0:T(8,128)S(1)} %bitcast_dynamic-update-slice_fusion.4, f32[]{:T(128)} %bitcast.104, f32[]{:T(128)} %bitcast.103, f32[]{:T(128)} %bitcast.102, f32[]{:T(128)} %bitcast.101, f32[]{:T(128)} %bitcast.100, f32[]{:T(128)} %bitcast.99, ...), kind=kLoop, calls=%fused_computation.225 | loop fusion | flops 1343488 | bytes 917588
  1049.7 17.6 %bitcast_dynamic-update-slice_fusion.2 = f32[9,8,8,512]{3,2,1,0:T(8,128)S(1)} fusion(f32[9,8,8,512]{3,2,1,0:T(8,128)S(1)} %bitcast_dynamic-update-slice_fusion.3, f32[]{:T(128)} %bitcast.112, f32[]{:T(128)} %bitcast.111, f32[]{:T(128)} %bitcast.110, f32[]{:T(128)} %bitcast.109, f32[]{:T(128)} %bitcast.108, f32[]{:T(128)} %bitcast.107, f32[]{:T(128)} %bitcast.106, ...), kind=kLoop, calls=%fused_computation.224 | loop fusion | flops 1802240 | bytes 1048688
  1067.4 22.6 %bitcast_dynamic-update-slice_fusion.1 = f32[9,8,8,512]{3,2,1,0:T(8,128)S(1)} fusion(f32[9,8,8,512]{3,2,1,0:T(8,128)S(1)} %bitcast_dynamic-update-slice_fusion.2, f32[]{:T(128)} %bitcast.121, f32[]{:T(128)} %bitcast.120, f32[]{:T(128)} %bitcast.119, f32[]{:T(128)} %bitcast.118, f32[]{:T(128)} %bitcast.117, f32[]{:T(128)} %bitcast.116, f32[]{:T(128)} %bitcast.115, ...), kind=kLoop, calls=%fused_computation.223 | loop fusion | flops 2326528 | bytes 1179792
  1090.0 28.5 %bitcast_dynamic-update-slice_fusion = f32[9,8,8,512]{3,2,1,0:T(8,128)S(1)} fusion(f32[9,8,8,512]{3,2,1,0:T(8,128)S(1)} %bitcast_dynamic-update-slice_fusion.1, f32[8,8,512]{2,1,0:T(8,128)S(1)} %copy-done.29, f32[]{:T(128)} %bitcast.131, f32[]{:T(128)} %bitcast.130, f32[]{:T(128)} %bitcast.129, f32[]{:T(128)} %bitcast.128, f32[]{:T(128)} %bitcast.127, ...), kind=kLoop, calls=%fused_computation.222 | loop fusion | flops 2883584 | bytes 1310900 | tf_op jit(solution)/shard_map/stack | solution.py:64
  (639 shorter events, 447.2 us)
Async XLA Ops:
  1.5 19.2 %collective-permute-start.2 = (f32[1,8,512]{2,1,0:T(8,128)S(1)}, f32[1,8,512]{2,1,0:T(8,128)S(1)}, u32[]{:S(2)}, u32[]{:S(2)}) collective-permute-start(f32[1,8,512]{2,1,0:T(8,128)S(1)} %get-tuple-element.65), channel_id=1, source_target_pairs={{0,8},{8,16},{16,24},{1,9},{9,17},{17,25},{2,10},{10,18},{18,26},{... | collective-permute-start | bytes 49160 | tf_op jit(solution)/shard_map/ppermute | solution.py:22
  6.4 15.9 %collective-permute-start = (f32[1,8,512]{2,1,0:T(8,128)S(1)}, f32[1,8,512]{2,1,0:T(8,128)S(1)}, u32[]{:S(2)}, u32[]{:S(2)}) collective-permute-start(f32[1,8,512]{2,1,0:T(8,128)S(1)} %get-tuple-element.64), channel_id=1, source_target_pairs={{8,0},{16,8},{24,16},{9,1},{17,9},{25,17},{10,2},{18,10},{26,18},{... | collective-permute-start | bytes 49160 | tf_op jit(solution)/shard_map/ppermute | solution.py:25
  8.5 22.5 %collective-permute-start.1 = (f32[1,8,512]{2,1,0:T(8,128)S(1)}, f32[1,8,512]{2,1,0:T(8,128)S(1)}, u32[]{:S(2)}, u32[]{:S(2)}) collective-permute-start(f32[1,8,512]{2,1,0:T(8,128)S(1)} %slice.920), channel_id=1, source_target_pairs={{0,8},{8,16},{16,24},{1,9},{9,17},{17,25},{2,10},{10,18},{18,26},{... | collective-permute-start | bytes 49160 | tf_op jit(solution)/shard_map/ppermute | solution.py:14
  13.9 17.0 %collective-permute-start.4 = (f32[8,1,512]{2,1,0:T(1,128)S(1)}, f32[8,1,512]{2,1,0:T(1,128)S(1)}, u32[]{:S(2)}, u32[]{:S(2)}) collective-permute-start(f32[8,1,512]{2,1,0:T(1,128)S(1)} %slice.926), channel_id=1, source_target_pairs={{0,1},{1,2},{2,3},{3,4},{4,5},{5,6},{6,7},{8,9},{9,10},{10,11},{11... | collective-permute-start | bytes 49160 | tf_op jit(solution)/shard_map/ppermute | solution.py:14
  22.3 8.6 collective-permute-start.3
  23.6 7.3 collective-permute-start.5
  33.1 6.4 collective-permute-start.6
  47.1 6.7 collective-permute-start.10
  48.4 6.2 collective-permute-start.11
  61.7 6.5 collective-permute-start.14
  69.0 6.6 collective-permute-start.16
  70.3 6.1 collective-permute-start.17
  77.7 6.5 collective-permute-start.18
  85.0 6.6 collective-permute-start.20
  93.7 6.6 collective-permute-start.22
  101.1 6.6 collective-permute-start.24
  109.7 7.1 collective-permute-start.26
  117.1 7.0 collective-permute-start.28
  118.4 6.4 collective-permute-start.29
  125.0 8.9 collective-permute-start.30
  126.3 7.6 collective-permute-start.31
  134.0 7.4 collective-permute-start.32
  135.3 6.5 collective-permute-start.33
  824.2 8.7 collective-permute-start.35
  (48 other events, 3868.6 us)
where the time goes:
time: 1130 us; the launch traced here: 1120 us
  other arithmetic  722 us (64%)
  local copies, waits for them, and re-layouts  139 us (12%)
  starting transfers between devices  122 us (11%)
  between operations  120 us (11%)
  waiting for transfers between devices  16.2 us (1%)
    reduce_sum x54, other arithmetic, triangle_of(): project = jnp.sum(matrix * reflector[None, :], axis=1)  232 us
    sub x48, other arithmetic, triangle_of(): matrix = matrix - 2.0 / weight * project[:, None] * reflector[None, :]  200 us
    sub x54, other arithmetic, triangle_of(): reflector = masked - alpha * (positions == column).astype(jnp.float32)  100 us
    slice x48, local copies, waits for them, and re-layouts, triangle_of(): current = matrix[column]  79.6 us
    ppermute x16, starting transfers between devices, padded_2(): lax.ppermute(lax.slice_in_dim(block, block.shape[dim] - width, None, axis...  75.4 us
    unnamed x8, other arithmetic  75.1 us
    reduce_sum x54, other arithmetic, triangle_of(): length = jnp.sqrt(jnp.sum(masked * masked))  37.8 us
    reduce_sum x54, other arithmetic, triangle_of(): weight = jnp.sum(reflector * reflector)  33.8 us
  transfers between devices with their start and end apart: 39, of which 18 were waited for; matrix products, arithmetic and copies ran while one was open for 1% of the time, Pallas kernels for 0%

commit v1 on v0

v1 whole, which is shorter than its diff:
```python
import functools
import math

import jax
import jax.numpy as jnp
from jax import lax
from jax.experimental import pallas as pl
from jax.experimental.pallas import tpu as pltpu
from jax.sharding import PartitionSpec as P

step_scale = 0.125
MESH = pl.DeviceIdType.MESH
LANES = 128
SUBLANES = 8
Y_UP, Y_DOWN, Z_UP, Z_DOWN = range(4)


def two_sum(a, b):
    total = a + b
    virtual = total - a
    return total, (a - (total - virtual)) + (b - virtual)


def split(a):
    scaled = a * 4097.0
    high = scaled - (scaled - a)
    return high, a - high


def two_product(a, b):
    product = a * b
    a_high, a_low = split(a)
    b_high, b_low = split(b)
    error = ((a_high * b_high - product) + a_high * b_low + a_low * b_high) + a_low * b_low
    return product, error


def pair_add(a, b):
    total, error = two_sum(a[0], b[0])
    return total, error + (a[1] + b[1])


def renormal(a):
    total = a[0] + a[1]
    return total, a[1] - (total - a[0])


def tree(parts):
    while len(parts) > 1:
        rest = parts[len(parts) // 2 * 2 :]
        parts = [pair_add(parts[i], parts[i + 1]) for i in range(0, len(parts) - 1, 2)] + rest
    return parts[0]


def kernel(
    count_y,
    count_z,
    root_cells,
    start,
    coef_x,
    coef_y,
    coef_z,
    shifts,
    out,
    triangle,
    basis,
    high,
    low,
    packed,
    halo,
    coef_pack,
    coef_halo,
    partial,
    gram,
    gather_z,
    gather_y,
    splat,
    send_sem,
    recv_sem,
    coef_send,
    coef_recv,
    z_send,
    z_recv,
    y_send,
    y_recv,
):
    rows_y, rows_z, length = start.shape
    depth = shifts.shape[0]
    count = depth + 1
    padded = gram.shape[0] // 2
    me_y, me_z = lax.axis_index("py"), lax.axis_index("pz")

    barrier = pltpu.get_barrier_semaphore()
    for away in range(1, count_z):
        pl.semaphore_signal(
            barrier, inc=1, device_id={"pz": lax.rem(me_z + away, count_z)}, device_id_type=MESH
        )
    for away in range(1, count_y):
        pl.semaphore_signal(
            barrier, inc=1, device_id={"py": lax.rem(me_y + away, count_y)}, device_id_type=MESH
        )

    partial[...] = jnp.zeros_like(partial)
    has = {
        Y_UP: me_y < count_y - 1,
        Y_DOWN: me_y > 0,
        Z_UP: me_z < count_z - 1,
        Z_DOWN: me_z > 0,
    }
    comes = {Y_UP: has[Y_DOWN], Y_DOWN: has[Y_UP], Z_UP: has[Z_DOWN], Z_DOWN: has[Z_UP]}
    target = {
        Y_UP: {"py": me_y + 1},
        Y_DOWN: {"py": me_y - 1},
        Z_UP: {"pz": me_z + 1},
        Z_DOWN: {"pz": me_z - 1},
    }

    def pack(value_row, y, slot):
        packed[0, slot, pl.ds(y, 1), :] = value_row[rows_z - 1 : rows_z, :]
        packed[1, slot, pl.ds(y, 1), :] = value_row[0:1, :]

    def keep(value_row, y, slot):
        basis[slot, y] = value_row
        value_high, value_low = split(value_row)
        high[slot, y] = value_high
        low[slot, y] = value_low

    for y in range(rows_y):
        row = start[y]
        keep(row, y, 0)
        pack(row, y, 0)
        coef_pack[pl.ds(y, 1), :] = coef_z[y, rows_z - 1 : rows_z, :]

    for way in range(4):

        @pl.when(jnp.logical_not(comes[way]))
        def _():
            halo[way] = jnp.zeros_like(halo[way])
            if way in (Y_UP, Z_UP):
                coef_halo[way // 2] = jnp.zeros_like(coef_halo[way // 2])

    pl.semaphore_wait(barrier, count_z + count_y - 2)

    def halo_copy(way, slot):
        source = {
            Y_UP: basis.at[slot, rows_y - 1],
            Y_DOWN: basis.at[slot, 0],
            Z_UP: packed.at[0, slot],
            Z_DOWN: packed.at[1, slot],
        }[way]
        return pltpu.make_async_remote_copy(
            src_ref=source,
            dst_ref=halo.at[way, slot],
            send_sem=send_sem.at[way, slot],
            recv_sem=recv_sem.at[way, slot],
            device_id=target[way],
            device_id_type=MESH,
        )

    def coef_copy(way):
        return pltpu.make_async_remote_copy(
            src_ref=coef_y.at[rows_y - 1] if way == Y_UP else coef_pack,
            dst_ref=coef_halo.at[way // 2],
            send_sem=coef_send.at[way // 2],
            recv_sem=coef_recv.at[way // 2],
            device_id=target[way],
            device_id_type=MESH,
        )

    for way in (Y_UP, Z_UP):
        pl.when(has[way])(lambda way=way: coef_copy(way).start())

    lane = lax.broadcasted_iota(jnp.int32, (rows_z, length), 1)
    sub = lax.broadcasted_iota(jnp.int32, (rows_z, length), 0)
    square_sub = lax.broadcasted_iota(jnp.int32, (padded, LANES), 0)
    square_lane = lax.broadcasted_iota(jnp.int32, (padded, LANES), 1)

    def gram_column(column, g_high, g_low):
        def pair(i, carry):
            total = None
            for y in range(rows_y):
                a_high, a_low = high[i, y], low[i, y]
                b_high, b_low = high[column, y], low[column, y]
                lead = a_high * b_high
                minor = (a_high * b_low + a_low * b_high) + a_low * b_low
                if total is None:
                    total = (lead, minor)
                else:
                    total = pair_add(total, (lead, minor))
            chunks = [
                (total[0][:, x : x + LANES], total[1][:, x : x + LANES])
                for x in range(0, length, LANES)
            ]
            s, e = tree(chunks)
            at = pl.multiple_of(i * SUBLANES, SUBLANES)
            partial[0, pl.ds(at, SUBLANES), :] = s
            partial[1, pl.ds(at, SUBLANES), :] = e
            return carry

        lax.fori_loop(0, column + 1, pair, 0)
        parts = [
            (
                partial[0, pl.ds(s, padded, stride=SUBLANES), :],
                partial[1, pl.ds(s, padded, stride=SUBLANES), :],
            )
            for s in range(SUBLANES)
        ]
        total = tree(parts)
        shift = LANES // 2
        while shift:
            total = pair_add(
                total, (pltpu.roll(total[0], shift, 1), pltpu.roll(total[1], shift, 1))
            )
            shift //= 2
        total = renormal(total)
        eye = square_sub == square_lane
        in_column = jnp.logical_and(square_lane == column, square_sub <= column)
        in_row = jnp.logical_and(square_sub == column, square_lane <= column)
        result = []
        for g, piece in ((g_high, total[0]), (g_low, total[1])):
            row = jnp.sum(jnp.where(eye, piece, 0.0), axis=0, keepdims=True)
            g = jnp.where(in_column, piece, g)
            g = jnp.where(in_row, row, g)
            result.append(g)
        return result

    def level(slot, grams):
        for way in range(4):
            pl.when(has[way])(lambda way=way: halo_copy(way, slot).start())
        grams = gram_column(slot, *grams)

        @pl.when(slot == 0)
        def _():
            for way in (Y_UP, Z_UP):
                pl.when(has[way])(lambda way=way: coef_copy(way).wait_send())
                pl.when(comes[way])(lambda way=way: coef_copy(way).wait_recv())

        for way in range(4):
            pl.when(has[way])(lambda way=way: halo_copy(way, slot).wait_send())
            pl.when(comes[way])(lambda way=way: halo_copy(way, slot).wait_recv())

        shift = shifts[slot]
        below_z = coef_halo[1] * (halo[Z_UP, slot] - packed[1, slot])
        flux_low = coef_halo[0] * (halo[Y_UP, slot] - basis[slot, 0])
        for y in range(rows_y):
            row = basis[slot, y]
            ahead = jnp.where(lane == length - 1, 0.0, pltpu.roll(row, length - 1, 1))
            flux_x = coef_x[y] * (row - ahead)
            image = flux_x - jnp.where(lane == 0, 0.0, pltpu.roll(flux_x, 1, 1))
            above = halo[Y_DOWN, slot] if y == rows_y - 1 else basis[slot, y + 1]
            flux_y = coef_y[y] * (row - above)
            image = image + flux_y
            image = image - flux_low
            flux_low = flux_y
            up = jnp.where(
                sub == rows_z - 1,
                halo[Z_DOWN, slot, pl.ds(y, 1), :],
                pltpu.roll(row, rows_z - 1, 0),
            )
            flux_z = coef_z[y] * (row - up)
            image = image + flux_z
            image = image - jnp.where(sub == 0, below_z[y : y + 1, :], pltpu.roll(flux_z, 1, 0))
            fresh = (image - shift * row) * step_scale
            keep(fresh, y, slot + 1)
            pack(fresh, y, slot + 1)
        return grams

    zero = jnp.zeros((padded, LANES), jnp.float32)
    grams = lax.fori_loop(0, depth, level, [zero, zero])
    g_high, g_low = gram_column(depth, *grams)

    def total_over(g, me, size, axis, buffer, sends, recvs):
        buffer[me] = gram[...]
        copies = []
        for away in range(1, size):
            copies.append(
                pltpu.make_async_remote_copy(
                    src_ref=gram,
                    dst_ref=buffer.at[me],
                    send_sem=sends.at[away - 1],
                    recv_sem=recvs.at[away - 1],
                    device_id={axis: lax.rem(me + away, size)},
                    device_id_type=MESH,
                )
            )
        for copy in copies:
            copy.start()
        for copy in copies:
            copy.wait()
        return renormal(
            tree([(buffer[i, :padded], buffer[i, padded:]) for i in range(size)])
        )

    gram[:padded] = g_high
    gram[padded:] = g_low
    g_high, g_low = total_over(gram, me_z, count_z, "pz", gather_z, z_send, z_recv)
    gram[:padded] = g_high
    gram[padded:] = g_low
    g_high, g_low = total_over(gram, me_y, count_y, "py", gather_y, y_send, y_recv)

    tri = zero
    row_lane = lax.broadcasted_iota(jnp.int32, (1, LANES), 1)
    for k in range(count):
        row_high, row_low = g_high[k : k + 1, :], g_low[k : k + 1, :]
        d_high = jnp.broadcast_to(row_high[:, k : k + 1], (1, LANES))
        d_low = jnp.broadcast_to(row_low[:, k : k + 1], (1, LANES))
        factor = jnp.where(row_lane >= k, row_high / jnp.sqrt(d_high) / root_cells, 0.0)
        tri = jnp.where(square_sub == k, factor, tri)
        unit = 1.0 / jnp.broadcast_to(factor[:, k : k + 1], (SUBLANES, LANES))
        splat[k * count + k] = unit
        for i in range(k + 1, count):
            splat[k * count + i] = jnp.broadcast_to(factor[:, i : i + 1], (SUBLANES, LANES))
        if k == count - 1:
            break
        inverse = 1.0 / d_high
        lead = row_high * inverse
        product, error = two_product(lead, d_high)
        minor = (((row_high - product) - error) + (row_low - lead * d_low)) * inverse
        col_high = jnp.broadcast_to(g_high[:, k : k + 1], (padded, LANES))
        col_low = jnp.broadcast_to(g_low[:, k : k + 1], (padded, LANES))
        lead = jnp.broadcast_to(lead, (padded, LANES))
        minor = jnp.broadcast_to(minor, (padded, LANES))
        product, error = two_product(col_high, lead)
        error = error + (col_high * minor + col_low * lead)
        total, rest = two_sum(g_high, -product)
        g_high, g_low = renormal((total, rest + (g_low - error)))
    triangle[...] = tri[:count, :count]

    def substitute(y, carry):
        for x in range(0, length, LANES):
            solved = []
            for i in range(count):
                value = basis[i, y, :, x : x + LANES]
                for k in range(i):
                    value = value - splat[k * count + i] * solved[k]
                value = value * splat[i * count + i]
                out[i, y, :, x : x + LANES] = value
                solved.append(value)
        return carry

    lax.fori_loop(0, rows_y, substitute, 0)


def on_device(start, coef_x, coef_y, coef_z, shifts):
    rows_y, rows_z, length = start.shape
    depth = shifts.shape[0]
    count = depth + 1
    padded = (count + SUBLANES - 1) // SUBLANES * SUBLANES
    count_y, count_z = lax.axis_size("py"), lax.axis_size("pz")
    cells = length * rows_y * rows_z * count_y * count_z
    whole = pl.BlockSpec(memory_space=pltpu.VMEM)
    face = (rows_z, length)
    pltpu_f32 = lambda *shape: pltpu.VMEM(shape, jnp.float32)
    dma = pltpu.SemaphoreType.DMA
    return pl.pallas_call(
        functools.partial(kernel, count_y, count_z, math.sqrt(cells)),
        out_shape=(
            jax.ShapeDtypeStruct((count, rows_y, rows_z, length), jnp.float32),
            jax.ShapeDtypeStruct((count, count), jnp.float32),
        ),
        in_specs=[whole] * 4 + [pl.BlockSpec(memory_space=pltpu.SMEM)],
        out_specs=(whole, whole),
        scratch_shapes=[
            pltpu_f32(count, rows_y, rows_z, length),
            pltpu_f32(count, rows_y, rows_z, length),
            pltpu_f32(count, rows_y, rows_z, length),
            pltpu_f32(2, count, rows_y, length),
            pltpu_f32(4, depth, *face),
            pltpu_f32(rows_y, length),
            pltpu_f32(2, *face),
            pltpu_f32(2, padded * SUBLANES, LANES),
            pltpu_f32(2 * padded, LANES),
            pltpu_f32(count_z, 2 * padded, LANES),
            pltpu_f32(count_y, 2 * padded, LANES),
            pltpu_f32(count * count, SUBLANES, LANES),
            dma((4, depth)),
            dma((4, depth)),
            dma((2,)),
            dma((2,)),
            dma((count_z - 1,)),
            dma((count_z - 1,)),
            dma((count_y - 1,)),
            dma((count_y - 1,)),
        ],
        compiler_params=pltpu.CompilerParams(collective_id=0, has_side_effects=True),
    )(start, coef_x, coef_y, coef_z, shifts)


def solution(mesh):
    placed = (
        P("py", "pz", None),
        P("py", "pz", None),
        P("py", "pz", None),
        P("py", "pz", None),
        P(),
    )
    return jax.shard_map(
        on_device,
        mesh=mesh,
        in_specs=placed,
        out_specs=(P(None, "py", "pz", None), P()),
        check_vma=False,
    )
```

time: 1130 us -> 46.4 us (0.04)
  other arithmetic: 722 us -> 0 us
  local copies, waits for them, and re-layouts: 139 us -> 2.97 us
  starting transfers between devices: 122 us -> 0 us
  between operations: 120 us -> 0.65 us
  Pallas kernels: 0 us -> 42.6 us
  waiting for transfers between devices: 16.2 us -> 0 us
    reduce_sum x162 -> x0, other arithmetic: 303 us -> none  [the longest x54 232 us: triangle_of(): project = jnp.sum(matrix * reflector[None, :], axis=1)]
    sub x102 -> x0, other arithmetic: 300 us -> none  [the longest x48 200 us: triangle_of(): matrix = matrix - 2.0 / weight * project[:, None] * reflector[None, :]]
    ppermute x39 -> x0, starting transfers between devices: 122 us -> none  [the longest x16 75.4 us: padded_2(): lax.ppermute(lax.slice_in_dim(block, block.shape[dim] - width, None, axis...]
    slice x127 -> x0, local copies, waits for them, and re-layouts: 120 us -> none  [the longest x48 79.6 us: triangle_of(): current = matrix[column]]
    unnamed x8 -> x0, other arithmetic: 75.1 us -> none
    pallas_call x0 -> x1, Pallas kernels: none -> 42.6 us  [on_device(): pl.pallas_call(functools.partial(kernel, count_y, count_z, math.sqrt(cell...]
    another operation x1 -> x0, other arithmetic: 28.5 us -> none  [forward(): return jnp.stack(solved)]
    ppermute x39 -> x0, waiting for transfers between devices: 16.2 us -> none  [the longest x16 8.76 us: padded_2(): lax.ppermute(lax.slice_in_dim(block, block.shape[dim] - width, None, axis...]
  transfers between devices with their start and end apart: 39 -> 0, of which waited for: 18 -> 0; matrix products, arithmetic and copies ran while one was open for 1% -> 0% of each run, Pallas kernels for 0% -> 0%
where the time goes in v1:
time: 46.4 us; the launch traced here: 46.2 us
  Pallas kernels  42.6 us (92%)
  local copies, waits for them, and re-layouts  2.97 us (6%)
  between operations  0.65 us (1%)
    pallas_call x1, Pallas kernels, on_device(): pl.pallas_call(functools.partial(kernel, count_y, count_z, math.sqrt(cell...  42.6 us
    unnamed x4, local copies, waits for them, and re-layouts  2.97 us

profile of v1, /device:TPU:0, one launch (start us, length us, event | category | flops | bytes accessed | tf_op | source)
XLA Modules:
  0.0 46.2 jit_solution(15736293995273024974)
XLA Ops:
  0.6 42.6 %shard_map.68 = (f32[9,8,8,512]{3,2,1,0:T(8,128)}, f32[9,9]{1,0:T(8,128)}) custom-call(f32[8,8,512]{2,1,0:T(8,128)} %start.1, f32[8,8,512]{2,1,0:T(8,128)} %coef_x.1, f32[8,8,512]{2,1,0:T(8,128)} %coef_y.1, f32[8,8,512]{2,1,0:T(8,128)} %coef_z.1, f32[8]{0:T(128)} %shifts.1), custom_call_target="tpu_custom_call" | custom-call | tf_op jit(solution)/shard_map/pallas_call | solution.py:355
  43.2 0.0 copy-start
  43.2 2.4 %copy.9 = f32[9,8,8,512]{3,2,1,0:T(8,128)} copy(f32[9,8,8,512]{3,2,1,0:T(8,128)} %get-tuple-element.4) | data formatting | bytes 2359296
  45.6 0.0 copy-done
  45.6 0.6 %copy.10 = f32[9,9]{1,0:T(8,128)} copy(f32[9,9]{1,0:T(8,128)S(1)} %copy-done) | data formatting | bytes 648
Async XLA Ops:
  43.2 2.4 %copy-start = (f32[9,9]{1,0:T(8,128)S(1)}, f32[9,9]{1,0:T(8,128)}, u32[]{:S(2)}) copy-start(f32[9,9]{1,0:T(8,128)} %get-tuple-element.5) | copy-start | bytes 976

commit v2 on v1

--- a/solution.py
+++ b/solution.py
@@ -52,29 +52,51 @@
     return parts[0]
 
 
+def wrap(high, low):
+    lane = lax.broadcasted_iota(jnp.int32, high.shape, 1)
+    return jnp.where(lane < LANES // 2, high, pltpu.roll(low, LANES // 2, 1))
+
+
+def unwrapped_sum(buffer):
+    parts = []
+    for i in range(buffer.shape[0]):
+        value = buffer[i]
+        parts.append((value, pltpu.roll(value, LANES // 2, 1)))
+    total = renormal(tree(parts))
+    lane = lax.broadcasted_iota(jnp.int32, total[0].shape, 1)
+    return [jnp.where(lane < LANES // 2, piece, 0.0) for piece in total]
+
+
 def kernel(
     count_y,
     count_z,
     root_cells,
-    start,
-    coef_x,
-    coef_y,
-    coef_z,
+    start_hbm,
+    x_hbm,
+    y_hbm,
+    z_hbm,
     shifts,
-    out,
+    basis_hbm,
     triangle,
     basis,
     high,
     low,
+    coef_x,
+    coef_y,
+    coef_z,
     packed,
     halo,
     coef_pack,
     coef_halo,
     partial,
-    gram,
-    gather_z,
-    gather_y,
-    splat,
+    early_source,
+    early_z,
+    early_y,
+    last_source,
+    last_z,
+    last_y,
+    load_sem,
+    store_sem,
     send_sem,
     recv_sem,
     coef_send,
@@ -84,10 +106,10 @@
     y_send,
     y_recv,
 ):
-    rows_y, rows_z, length = start.shape
     depth = shifts.shape[0]
     count = depth + 1
-    padded = gram.shape[0] // 2
+    rows_y, rows_z, length = coef_x.shape
+    padded = triangle.shape[0]
     me_y, me_z = lax.axis_index("py"), lax.axis_index("pz")
 
     barrier = pltpu.get_barrier_semaphore()
@@ -100,6 +122,19 @@
             barrier, inc=1, device_id={"py": lax.rem(me_y + away, count_y)}, device_id_type=MESH
         )
 
+    loads = [
+        pltpu.make_async_copy(source, target, load_sem.at[i])
+        for i, (source, target) in enumerate(
+            (
+                (start_hbm, basis.at[0]),
+                (z_hbm, coef_z),
+                (y_hbm, coef_y),
+                (x_hbm, coef_x),
+            )
+        )
+    ]
+    for load in loads:
+        load.start()
     partial[...] = jnp.zeros_like(partial)
     has = {
         Y_UP: me_y < count_y - 1,
@@ -120,16 +155,9 @@
         packed[1, slot, pl.ds(y, 1), :] = value_row[0:1, :]
 
     def keep(value_row, y, slot):
-        basis[slot, y] = value_row
         value_high, value_low = split(value_row)
         high[slot, y] = value_high
         low[slot, y] = value_low
-
-    for y in range(rows_y):
-        row = start[y]
-        keep(row, y, 0)
-        pack(row, y, 0)
-        coef_pack[pl.ds(y, 1), :] = coef_z[y, rows_z - 1 : rows_z, :]
 
     for way in range(4):
 
@@ -139,6 +167,14 @@
             if way in (Y_UP, Z_UP):
                 coef_halo[way // 2] = jnp.zeros_like(coef_halo[way // 2])
 
+    loads[0].wait()
+    loads[1].wait()
+    for y in range(rows_y):
+        row = basis[0, y]
+        keep(row, y, 0)
+        pack(row, y, 0)
+        coef_pack[pl.ds(y, 1), :] = coef_z[y, rows_z - 1 : rows_z, :]
+    loads[2].wait()
     pl.semaphore_wait(barrier, count_z + count_y - 2)
 
     def halo_copy(way, slot):
@@ -166,9 +202,6 @@
             device_id=target[way],
             device_id_type=MESH,
         )
-
-    for way in (Y_UP, Z_UP):
-        pl.when(has[way])(lambda way=way: coef_copy(way).start())
 
     lane = lax.broadcasted_iota(jnp.int32, (rows_z, length), 1)
     sub = lax.broadcasted_iota(jnp.int32, (rows_z, length), 0)
@@ -224,13 +257,50 @@
             result.append(g)
         return result
 
-    def level(slot, grams):
+    def store(slot):
+        return pltpu.make_async_copy(basis.at[slot], basis_hbm.at[slot], store_sem.at[slot])
+
+    def exchange(source, buffer, me, size, axis, sends, recvs, stage):
+        return [
+            pltpu.make_async_remote_copy(
+                src_ref=source,
+                dst_ref=buffer.at[me],
+                send_sem=sends.at[stage, away - 1],
+                recv_sem=recvs.at[stage, away - 1],
+                device_id={axis: lax.rem(me + away, size)},
+                device_id_type=MESH,
+            )
+            for away in range(1, size)
+        ]
+
+    def begin(copies, source, buffer, me, value):
+        source[...] = value
+        buffer[me] = value
+        for copy in copies:
+            copy.start()
+
+    def end(copies, buffer):
+        for copy in copies:
+            copy.wait()
+        return unwrapped_sum(buffer)
+
+    early_z_copies = exchange(early_source.at[0], early_z, me_z, count_z, "pz", z_send, z_recv, 0)
+    early_y_copies = exchange(early_source.at[1], early_y, me_y, count_y, "py", y_send, y_recv, 0)
+    last_z_copies = exchange(last_source.at[0], last_z, me_z, count_z, "pz", z_send, z_recv, 1)
+    last_y_copies = exchange(last_source.at[1], last_y, me_y, count_y, "py", y_send, y_recv, 1)
+
+    def level(slot, grams, first=False, hook=None):
         for way in range(4):
             pl.when(has[way])(lambda way=way: halo_copy(way, slot).start())
+        if first:
+            for way in (Y_UP, Z_UP):
+                pl.when(has[way])(lambda way=way: coef_copy(way).start())
+        store(slot).start()
         grams = gram_column(slot, *grams)
-
-        @pl.when(slot == 0)
-        def _():
+        if hook is not None:
+            hook(grams)
+        if first:
+            loads[3].wait()
             for way in (Y_UP, Z_UP):
                 pl.when(has[way])(lambda way=way: coef_copy(way).wait_send())
                 pl.when(comes[way])(lambda way=way: coef_copy(way).wait_recv())
@@ -261,42 +331,45 @@
             image = image + flux_z
             image = image - jnp.where(sub == 0, below_z[y : y + 1, :], pltpu.roll(flux_z, 1, 0))
             fresh = (image - shift * row) * step_scale
+            basis[slot + 1, y] = fresh
             keep(fresh, y, slot + 1)
             pack(fresh, y, slot + 1)
         return grams
 
+    def early_first(grams):
+        begin(early_z_copies, early_source.at[0], early_z, me_z, wrap(*grams))
+
+    def early_second(grams):
+        total = end(early_z_copies, early_z)
+        begin(early_y_copies, early_source.at[1], early_y, me_y, wrap(*total))
+
     zero = jnp.zeros((padded, LANES), jnp.float32)
-    grams = lax.fori_loop(0, depth, level, [zero, zero])
-    g_high, g_low = gram_column(depth, *grams)
-
-    def total_over(g, me, size, axis, buffer, sends, recvs):
-        buffer[me] = gram[...]
-        copies = []
-        for away in range(1, size):
-            copies.append(
-                pltpu.make_async_remote_copy(
-                    src_ref=gram,
-                    dst_ref=buffer.at[me],
-                    send_sem=sends.at[away - 1],
-                    recv_sem=recvs.at[away - 1],
-                    device_id={axis: lax.rem(me + away, size)},
-                    device_id_type=MESH,
-                )
-            )
-        for copy in copies:
-            copy.start()
-        for copy in copies:
-            copy.wait()
-        return renormal(
-            tree([(buffer[i, :padded], buffer[i, padded:]) for i in range(size)])
-        )
-
-    gram[:padded] = g_high
-    gram[padded:] = g_low
-    g_high, g_low = total_over(gram, me_z, count_z, "pz", gather_z, z_send, z_recv)
-    gram[:padded] = g_high
-    gram[padded:] = g_low
-    g_high, g_low = total_over(gram, me_y, count_y, "py", gather_y, y_send, y_recv)
+    grams = level(0, [zero, zero], first=True)
+    grams = lax.fori_loop(1, depth - 2, level, grams)
+    grams = level(depth - 2, grams, hook=early_first)
+    grams = level(depth - 1, grams, hook=early_second)
+    store(depth).start()
+    grams = gram_column(depth, *grams)
+
+    tile_sub = lax.broadcasted_iota(jnp.int32, (SUBLANES, LANES), 0)
+    tail = [
+        jnp.where(tile_sub == 0, g[depth - 1 : depth, :], jnp.where(tile_sub == 1, g[depth:count, :], 0.0))
+        for g in grams
+    ]
+    begin(last_z_copies, last_source.at[0], last_z, me_z, wrap(*tail))
+    tail = end(last_z_copies, last_z)
+    begin(last_y_copies, last_source.at[1], last_y, me_y, wrap(*tail))
+    head = end(early_y_copies, early_y)
+    tail = end(last_y_copies, last_y)
+    eye = square_sub == square_lane
+    grams = []
+    for g, rows in zip(head, tail):
+        for k, row in ((depth - 1, rows[0:1, :]), (depth, rows[1:2, :])):
+            column = jnp.sum(jnp.where(eye, row, 0.0), axis=1, keepdims=True)
+            g = jnp.where(square_lane == k, column, g)
+            g = jnp.where(square_sub == k, row, g)
+        grams.append(g)
+    g_high, g_low = grams
 
     tri = zero
     row_lane = lax.broadcasted_iota(jnp.int32, (1, LANES), 1)
@@ -306,10 +379,6 @@
         d_low = jnp.broadcast_to(row_low[:, k : k + 1], (1, LANES))
         factor = jnp.where(row_lane >= k, row_high / jnp.sqrt(d_high) / root_cells, 0.0)
         tri = jnp.where(square_sub == k, factor, tri)
-        unit = 1.0 / jnp.broadcast_to(factor[:, k : k + 1], (SUBLANES, LANES))
-        splat[k * count + k] = unit
-        for i in range(k + 1, count):
-            splat[k * count + i] = jnp.broadcast_to(factor[:, i : i + 1], (SUBLANES, LANES))
         if k == count - 1:
             break
         inverse = 1.0 / d_high
@@ -324,9 +393,24 @@
         error = error + (col_high * minor + col_low * lead)
         total, rest = two_sum(g_high, -product)
         g_high, g_low = renormal((total, rest + (g_low - error)))
-    triangle[...] = tri[:count, :count]
-
-    def substitute(y, carry):
+    triangle[...] = tri
+    for slot in range(count):
+        store(slot).wait()
+
+
+def substitute(basis, factor, out, triangle, splat):
+    count, rows_y, rows_z, length = basis.shape
+
+    @pl.when(pl.program_id(0) == 0)
+    def _():
+        tri = factor[...]
+        triangle[...] = tri[:count, :count]
+        for k in range(count):
+            for i in range(k, count):
+                value = jnp.broadcast_to(tri[k : k + 1, i : i + 1], (SUBLANES, LANES))
+                splat[k * count + i] = 1.0 / value if i == k else value
+
+    def plane(y, carry):
         for x in range(0, length, LANES):
             solved = []
             for i in range(count):
@@ -338,7 +422,7 @@
                 solved.append(value)
         return carry
 
-    lax.fori_loop(0, rows_y, substitute, 0)
+    lax.fori_loop(0, rows_y, plane, 0)
 
 
 def on_device(start, coef_x, coef_y, coef_z, shifts):
@@ -352,38 +436,59 @@
     face = (rows_z, length)
     pltpu_f32 = lambda *shape: pltpu.VMEM(shape, jnp.float32)
     dma = pltpu.SemaphoreType.DMA
-    return pl.pallas_call(
+    anywhere = pl.BlockSpec(memory_space=pl.ANY)
+    basis, factor = pl.pallas_call(
         functools.partial(kernel, count_y, count_z, math.sqrt(cells)),
         out_shape=(
             jax.ShapeDtypeStruct((count, rows_y, rows_z, length), jnp.float32),
-            jax.ShapeDtypeStruct((count, count), jnp.float32),
+            jax.ShapeDtypeStruct((padded, LANES), jnp.float32),
         ),
-        in_specs=[whole] * 4 + [pl.BlockSpec(memory_space=pltpu.SMEM)],
-        out_specs=(whole, whole),
+        in_specs=[anywhere] * 4 + [pl.BlockSpec(memory_space=pltpu.SMEM)],
+        out_specs=(anywhere, whole),
         scratch_shapes=[
             pltpu_f32(count, rows_y, rows_z, length),
             pltpu_f32(count, rows_y, rows_z, length),
             pltpu_f32(count, rows_y, rows_z, length),
+            pltpu_f32(rows_y, rows_z, length),
+            pltpu_f32(rows_y, rows_z, length),
+            pltpu_f32(rows_y, rows_z, length),
             pltpu_f32(2, count, rows_y, length),
             pltpu_f32(4, depth, *face),
             pltpu_f32(rows_y, length),
             pltpu_f32(2, *face),
             pltpu_f32(2, padded * SUBLANES, LANES),
-            pltpu_f32(2 * padded, LANES),
-            pltpu_f32(count_z, 2 * padded, LANES),
-            pltpu_f32(count_y, 2 * padded, LANES),
-            pltpu_f32(count * count, SUBLANES, LANES),
+            pltpu_f32(2, padded, LANES),
+            pltpu_f32(count_z, padded, LANES),
+            pltpu_f32(count_y, padded, LANES),
+            pltpu_f32(2, SUBLANES, LANES),
+            pltpu_f32(count_z, SUBLANES, LANES),
+            pltpu_f32(count_y, SUBLANES, LANES),
+            dma((4,)),
+            dma((count,)),
             dma((4, depth)),
             dma((4, depth)),
             dma((2,)),
             dma((2,)),
-            dma((count_z - 1,)),
-            dma((count_z - 1,)),
-            dma((count_y - 1,)),
-            dma((count_y - 1,)),
+            dma((2, count_z - 1)),
+            dma((2, count_z - 1)),
+            dma((2, count_y - 1)),
+            dma((2, count_y - 1)),
         ],
         compiler_params=pltpu.CompilerParams(collective_id=0, has_side_effects=True),
     )(start, coef_x, coef_y, coef_z, shifts)
+    block = (count, max(1, rows_y // 4), rows_z, length)
+    planes = pl.BlockSpec(block, lambda i: (0, i, 0, 0))
+    return pl.pallas_call(
+        substitute,
+        grid=(rows_y // block[1],),
+        out_shape=(
+            jax.ShapeDtypeStruct((count, rows_y, rows_z, length), jnp.float32),
+            jax.ShapeDtypeStruct((count, count), jnp.float32),
+        ),
+        in_specs=[planes, pl.BlockSpec((padded, LANES), lambda i: (0, 0))],
+        out_specs=(planes, pl.BlockSpec((count, count), lambda i: (0, 0))),
+        scratch_shapes=[pltpu_f32(count * count, SUBLANES, LANES)],
+    )(basis, factor)
 
 
 def solution(mesh):

time: 46.4 us -> 45.8 us (0.987)
  local copies, waits for them, and re-layouts: 2.97 us -> 0 us
  Pallas kernels: 42.6 us -> 45 us
    pallas_call x0 -> x1, Pallas kernels: none -> 3.81 us  [on_device(): pl.pallas_call(substitute, grid=(rows_y // block[1],), out_shape=(jax.Sha...]
    unnamed x4 -> x0, local copies, waits for them, and re-layouts: 2.97 us -> none
    pallas_call x1, Pallas kernels: 42.6 us -> 41.2 us  [on_device(): pl.pallas_call(functools.partial(kernel, count_y, count_z, math.sqrt(cell...]
where the time goes in v2:
time: 45.8 us; the launch traced here: 45.6 us
  Pallas kernels  45 us (98%)
  between operations  0.64 us (1%)
    pallas_call x1, Pallas kernels, on_device(): pl.pallas_call(functools.partial(kernel, count_y, count_z, math.sqrt(cell...  41.2 us
    pallas_call x1, Pallas kernels, on_device(): pl.pallas_call(substitute, grid=(rows_y // block[1],), out_shape=(jax.Sha...  3.81 us

profile of v2, /device:TPU:0, one launch (start us, length us, event | category | flops | bytes accessed | tf_op | source)
XLA Modules:
  0.0 45.6 jit_solution(9439097917078557883)
XLA Ops:
  0.6 41.2 %shard_map.68 = (f32[9,8,8,512]{3,2,1,0:T(8,128)}, f32[16,128]{1,0:T(8,128)}) custom-call(f32[8,8,512]{2,1,0:T(8,128)} %start_hbm.1, f32[8,8,512]{2,1,0:T(8,128)} %x_hbm.1, f32[8,8,512]{2,1,0:T(8,128)} %y_hbm.1, f32[8,8,512]{2,1,0:T(8,128)} %z_hbm.1, f32[8]{0:T(128)} %shifts.1), custom_call_target="tpu_custom_call" | custom-call | tf_op jit(solution)/shard_map/pallas_call | solution.py:440
  41.8 3.8 %shard_map.69 = (f32[9,8,8,512]{3,2,1,0:T(8,128)}, f32[9,9]{1,0:T(8,128)}) custom-call(f32[9,8,8,512]{3,2,1,0:T(8,128)} %get-tuple-element.4.basis, f32[16,128]{1,0:T(8,128)} %get-tuple-element.5.factor), custom_call_target="tpu_custom_call" | custom-call | tf_op jit(solution)/shard_map/pallas_call | solution.py:481
